TPU v7x, 256 devices: a whole 4x4x8 slice. The times are simulated.
256 devices in a mesh: col: 64 (over y, z, core), row: 4 (over x).
Axes of the slice: x: 4, y: 4, z: 8, core: 2. Of those that a mesh axis runs over, the one named last changes fastest.
Arguments:
- r_slab: float32 [1024, 16384], P('row', 'col'), may hold values from -4 to 8, as said below
- arc_rows: float32 [4096, 16384], P('row', 'col'), may hold values from -6 to 6
- arc_blocks: int32 [32, 64], P('row', 'col'), may hold values 0 or 1
Outputs:
- r_updated: float32 [1024, 16384], P('row', 'col')
Inputs may be any that keep to these rules, and one draw needn't show every extreme that they name: r_slab is zero wherever an entry's global column index is below its row index, and its diagonal is positive.
All inputs are finite; a program needn't handle non-finite values. No bound on the sum of `arc_blocks` on one device may be relied on, other than what follows from the above.
Results may differ from a plain program's by a relative error of at most 0.000098.
Values sent between devices are 32-bit elements; how exact they have to be, the bound alone decides.
A program may use at most 64 MiB of HBM per device.

v0:
```python
import jax
import jax.numpy as jnp
from jax import lax
from jax.sharding import PartitionSpec as P

B = 256
P_SIZE = 4
ARC_ROWS = 128
HI = lax.Precision.HIGHEST


def inner_dot(left, right):
    return lax.dot_general(left, right, (((0,), (0,)), ((), ())), precision=HI)


def plain_dot(left, right):
    return jnp.dot(left, right, precision=HI)


def on_device(r_slab, arc_rows, arc_blocks):
    n_col = lax.axis_size("col")
    col_index = lax.axis_index("col")
    row_index = lax.axis_index("row")
    n_arcs, blocks_here = arc_blocks.shape
    lead = P_SIZE * B
    live = arc_blocks.astype(jnp.float32)
    masked = (arc_rows.reshape(n_arcs, ARC_ROWS, blocks_here, B) * live[:, None, :, None]).reshape(
        arc_rows.shape
    )
    stacked = jnp.concatenate([r_slab, masked], axis=0)
    height = stacked.shape[0]
    part = height // n_col
    pieces = stacked.reshape(n_col, part, B)
    pieces = lax.all_to_all(pieces, "col", split_axis=0, concat_axis=0, tiled=True)
    mine = pieces[:P_SIZE]
    panels = lax.all_gather(mine, "col")
    panels = panels.transpose(0, 2, 1, 3).reshape(height, lead)
    share = lead // n_col
    own = lax.dynamic_slice(panels, (0, col_index * share), (height, share))
    gram_part = lax.psum(inner_dot(own, panels), "row")
    gram = lax.all_gather(gram_part, "col", tiled=True)
    rhs = lax.psum(inner_dot(panels, stacked), "row")
    lower = jnp.linalg.cholesky(gram, symmetrize_input=False)
    factor = jax.scipy.linalg.solve_triangular(lower, rhs, lower=True)
    mine_out = lax.dynamic_slice(factor, (row_index * B, 0), (B, B))
    row_ids = row_index * B + lax.broadcasted_iota(jnp.int32, (B, B), 0)
    col_ids = col_index * B + lax.broadcasted_iota(jnp.int32, (B, B), 1)
    return jnp.where(col_ids >= row_ids, mine_out, jnp.zeros_like(mine_out))


def solution(mesh):
    return jax.shard_map(
        on_device,
        mesh=mesh,
        in_specs=(P("row", "col"), P("row", "col"), P("row", "col")),
        out_specs=P("row", "col"),
        check_vma=False,
    )
```

profile of v0, /device:TPU:1, one launch (start us, length us, event | category | flops | bytes accessed | tf_op | source)
XLA Modules:
  0.0 636.5 jit_solution(12063077370027670616)
XLA Ops:
  7.3 1.4 broadcast_multiply_fusion
  8.7 2.1 pad_maximum_fusion
  10.8 1.4 reshape.90
  12.2 52.7 %all_to_all.5 = f32[64,20,256]{2,1,0:T(8,128)S(1)} all-to-all(f32[64,20,256]{2,1,0:T(8,128)S(1)} %reshape.90), channel_id=1, replica_groups=mesh['col'=64,'row'=4] {'col'}, dimensions={0} | all-to-all | bytes 2621440 | tf_op jit(solution)/shard_map/all_to_all | solution.py:34
  65.7 78.4 %all-gather.6.cloned.1.call-done = f32[256,20,256]{2,1,0:T(8,128)} async-done(((f32[4,20,256]{2,1,0:T(8,128)}), f32[256,20,256]{2,1,0:T(8,128)}) %all-gather.6.cloned.1.call-update) | async-done | bytes 5242896 | tf_op jit(solution)/shard_map/all_gather | solution.py:36
  144.1 5.2 copy.5
  149.2 1.3 copy.6
  150.5 9.5 %fusion.63 = f32[1024,256]{1,0:T(8,128)} fusion(f32[1280,1024]{1,0:T(8,128)S(1)} %bitcast.108, f32[1024,256]{1,0:T(8,128)S(1)} %broadcast_multiply_fusion, f32[256,256]{1,0:T(8,128)S(1)} %copy-done), kind=kOutput, calls=%fused_computation.162 | convolution fusion | flops 4026859520 | bytes 7602176 | tf_op jit(solution)/shard_map/dot_general | solution.py:13
  160.1 14.3 %fusion.5 = f32[16,1024]{1,0:T(8,128)} fusion(f32[1280,1024]{1,0:T(8,128)S(1)} %bitcast.109, s32[]{:T(128)S(6)} %select_n.14), kind=kOutput, calls=%fused_computation.31 | convolution fusion | flops 251658240 | bytes 5963780 | tf_op jit(solution)/shard_map/dot_general | solution.py:13
  174.4 46.4 %all-reduce.4.cloned.1.call-done = (f32[1024,256]{1,0:T(8,128)}, f32[16,1024]{1,0:T(8,128)}) async-done(((f32[1024,256]{1,0:T(8,128)}, f32[16,1024]{1,0:T(8,128)}), (f32[1024,256]{1,0:T(8,128)}, f32[16,1024]{1,0:T(8,128)})) %all-reduce.4.cloned.1.call-update) | async-done | bytes 1114128 | tf_op jit(solution)/shard_map/psum | solution.py:42
  220.8 84.7 %all-gather.4.cloned.1.call-done = f32[1024,1024]{1,0:T(8,128)} async-done(((f32[16,1024]{1,0:T(8,128)}), f32[1024,1024]{1,0:T(8,128)}) %all-gather.4.cloned.1.call-update) | async-done | bytes 4194320 | tf_op jit(solution)/shard_map/all_gather | solution.py:41
  305.5 0.8 cholesky.580
  306.4 11.7 %cholesky.223 = f32[128,128]{1,0:T(8,128)S(1)} custom-call(f32[128,128]{1,0:T(8,128)S(1)} %cholesky.580), custom_call_target="Cholesky" | custom-call | tf_op jit(solution)/shard_map/jit(cholesky)/cholesky | solution.py:43
  318.1 9.8 %custom-call.63 = f32[1,128,128]{1,2,0:T(8,128)S(1)} custom-call(f32[1,128,128]{2,1,0:T(8,128)S(1)} %get-tuple-element.71), custom_call_target="InvertDiagBlocksLowerTriangular" | custom-call | tf_op jit(solution)/shard_map/jit(cholesky)/cholesky | solution.py:43
  328.0 2.5 cholesky.255
  330.5 2.4 constant_dynamic-update-slice_fusion.31
  332.8 1.5 convolution_subtract_fusion
  334.4 11.7 %cholesky.244 = f32[128,128]{1,0:T(8,128)S(1)} custom-call(f32[128,128]{1,0:T(8,128)S(1)} %cholesky.584), custom_call_target="Cholesky" | custom-call | tf_op jit(solution)/shard_map/jit(cholesky)/cholesky | solution.py:43
  346.8 10.2 %custom-call.64 = f32[1,128,128]{1,2,0:T(8,128)S(1)} custom-call(f32[1,128,128]{2,1,0:T(8,128)S(1)} %get-tuple-element.68), custom_call_target="InvertDiagBlocksLowerTriangular" | custom-call | tf_op jit(solution)/shard_map/jit(cholesky)/cholesky | solution.py:43
  356.9 1.2 convolution_dynamic-update-slice_fusion
  358.2 2.1 convolution_subtract_fusion.1
  360.3 11.7 %cholesky.468 = f32[128,128]{1,0:T(8,128)S(1)} custom-call(f32[128,128]{1,0:T(8,128)S(1)} %cholesky.589), custom_call_target="Cholesky" | custom-call | tf_op jit(solution)/shard_map/jit(cholesky)/cholesky | solution.py:43
  372.6 0.7 compare_reduce_fusion.5
  373.4 9.8 %custom-call.65 = f32[1,128,128]{1,2,0:T(8,128)S(1)} custom-call(f32[1,128,128]{2,1,0:T(8,128)S(1)} %get-tuple-element.65), custom_call_target="InvertDiagBlocksLowerTriangular" | custom-call | tf_op jit(solution)/shard_map/jit(cholesky)/cholesky | solution.py:43
  383.2 1.2 convolution_dynamic-update-slice_fusion.1
  384.3 2.3 convolution_subtract_fusion.2
  386.7 11.9 %cholesky.487 = f32[128,128]{1,0:T(8,128)S(1)} custom-call(f32[128,128]{1,0:T(8,128)S(1)} %cholesky.594), custom_call_target="Cholesky" | custom-call | tf_op jit(solution)/shard_map/jit(cholesky)/cholesky | solution.py:43
  399.9 9.8 %custom-call.66 = f32[1,128,128]{1,2,0:T(8,128)S(1)} custom-call(f32[1,128,128]{2,1,0:T(8,128)S(1)} %get-tuple-element.62), custom_call_target="InvertDiagBlocksLowerTriangular" | custom-call | tf_op jit(solution)/shard_map/jit(cholesky)/cholesky | solution.py:43
  409.7 1.1 convolution_dynamic-update-slice_fusion.2
  410.8 2.3 convolution_subtract_fusion.3
  413.2 11.7 %cholesky.506 = f32[128,128]{1,0:T(8,128)S(1)} custom-call(f32[128,128]{1,0:T(8,128)S(1)} %cholesky.599), custom_call_target="Cholesky" | custom-call | tf_op jit(solution)/shard_map/jit(cholesky)/cholesky | solution.py:43
  425.5 0.7 compare_reduce_fusion.3
  426.2 9.8 %custom-call.67 = f32[1,128,128]{1,2,0:T(8,128)S(1)} custom-call(f32[1,128,128]{2,1,0:T(8,128)S(1)} %get-tuple-element.59), custom_call_target="InvertDiagBlocksLowerTriangular" | custom-call | tf_op jit(solution)/shard_map/jit(cholesky)/cholesky | solution.py:43
  436.0 1.0 convolution_dynamic-update-slice_fusion.3
  437.1 2.5 convolution_subtract_fusion.4
  439.6 11.7 %cholesky.526 = f32[128,128]{1,0:T(8,128)S(1)} custom-call(f32[128,128]{1,0:T(8,128)S(1)} %cholesky.604), custom_call_target="Cholesky" | custom-call | tf_op jit(solution)/shard_map/jit(cholesky)/cholesky | solution.py:43
  452.7 9.8 %custom-call.68 = f32[1,128,128]{1,2,0:T(8,128)S(1)} custom-call(f32[1,128,128]{2,1,0:T(8,128)S(1)} %get-tuple-element.56), custom_call_target="InvertDiagBlocksLowerTriangular" | custom-call | tf_op jit(solution)/shard_map/jit(cholesky)/cholesky | solution.py:43
  462.5 0.9 convolution_dynamic-update-slice_fusion.5
  463.4 2.0 convolution_subtract_fusion.11
  465.5 11.7 %cholesky.546 = f32[128,128]{1,0:T(8,128)S(1)} custom-call(f32[128,128]{1,0:T(8,128)S(1)} %cholesky.609), custom_call_target="Cholesky" | custom-call | tf_op jit(solution)/shard_map/jit(cholesky)/cholesky | solution.py:43
  478.5 10.2 %custom-call.69 = f32[1,128,128]{1,2,0:T(8,128)S(1)} custom-call(f32[1,128,128]{2,1,0:T(8,128)S(1)} %get-tuple-element.53), custom_call_target="InvertDiagBlocksLowerTriangular" | custom-call | tf_op jit(solution)/shard_map/jit(cholesky)/cholesky | solution.py:43
  488.6 0.8 convolution_dynamic-update-slice_fusion.6
  489.5 1.8 convolution_subtract_fusion.13
  491.3 11.7 %cholesky.564 = f32[128,128]{1,0:T(8,128)S(1)} custom-call(f32[128,128]{1,0:T(8,128)S(1)} %convolution_subtract_fusion.13), custom_call_target="Cholesky" | custom-call | tf_op jit(solution)/shard_map/jit(cholesky)/cholesky | solution.py:43
  503.6 0.7 compare_reduce_fusion
  510.1 4.9 select_select_fusion
  515.0 23.1 %while.1 = (s32[]{:T(128)}, f32[1024,1024]{1,0:T(8,128)}, s32[8,2]{0,1:T(2,128)S(1)}, f32[8,128,128]{2,1,0:T(8,128)S(1)}, s32[]{:T(128)}) while((s32[]{:T(128)}, f32[1024,1024]{1,0:T(8,128)}, s32[8,2]{0,1:T(2,128)S(1)}, f32[8,128,128]{2,1,0:T(8,128)S(1)}, s32[]{:T(128)}) %tuple.58), condition=%wide.while_cond, body=%wide.while_body.sunk | while | flops 2 | bytes 131181 | solution.py:44
  515.7 2.3 bitcast_dynamic-update-slice_fusion.2
  518.6 2.3 bitcast_dynamic-update-slice_fusion.2
  521.5 2.3 bitcast_dynamic-update-slice_fusion.2
  524.4 2.3 bitcast_dynamic-update-slice_fusion.2
  527.3 2.3 bitcast_dynamic-update-slice_fusion.2
  530.2 2.3 bitcast_dynamic-update-slice_fusion.2
  533.0 2.3 bitcast_dynamic-update-slice_fusion.2
  535.9 2.2 bitcast_dynamic-update-slice_fusion.2
  538.1 78.6 %custom-call.70 = f32[8,128,128]{1,2,0:T(8,128)S(1)} custom-call(f32[8,128,128]{2,1,0:T(8,128)S(1)} %get-tuple-element.12), custom_call_target="InvertDiagBlocksLowerTriangular" | custom-call | tf_op jit(solution)/shard_map/jit(_solve_triangular)/triangular_solve | solution.py:44
  617.1 1.1 convolution_subtract_fusion.10
  618.5 1.2 convolution_subtract_fusion.8
  620.0 1.3 convolution_subtract_fusion.7
  621.7 1.4 convolution_subtract_fusion.6
  623.4 1.5 convolution_subtract_fusion.5
  625.2 1.5 convolution_subtract_fusion.9
  627.0 1.6 convolution_subtract_fusion.12
  629.0 0.8 dynamic-slice_select_fusion
  (59 shorter events, 16.1 us)
Async XLA Ops:
  6.5 137.5 %all-gather.6.cloned.1.call-start = ((), (), s32[]{:S(2)}) async-start(), calls=%async_computation.2 | async-start | bytes 6389760 | tf_op jit(solution)/shard_map/all_gather | solution.py:36
  65.6 155.2 %all-reduce.4.cloned.1.call-start = ((), (), s32[]{:S(2)}) async-start(), calls=%async_computation.3 | async-start | bytes 2228224 | tf_op jit(solution)/shard_map/psum | solution.py:42
  149.2 1.3 copy-start
  174.4 131.2 %all-gather.4.cloned.1.call-start = ((), (), s32[]{:S(2)}) async-start(), calls=%async_computation.1 | async-start | bytes 4259840 | tf_op jit(solution)/shard_map/all_gather | solution.py:41
  510.1 106.6 %copy-start.1 = (f32[1024,256]{1,0:T(8,128)S(1)}, f32[1024,256]{1,0:T(8,128)}, u32[]{:S(2)}) copy-start(f32[1024,256]{1,0:T(8,128)} %get-tuple-element.21) | copy-start | bytes 3145732
Sparse Core Ops, SparseCore 0:
  65.7 78.2 all-gather.5
  174.5 46.2 all-reduce.3
  223.9 81.5 all-gather.3
where the time goes:
time: 647 us; the launch traced here: 636 us
  other arithmetic  261 us (40%)
  waiting for transfers between devices  210 us (32%)
  matrix products  59.2 us (9%)
  blocking collectives  52.7 us (8%)
  local copies, waits for them, and re-layouts  34.8 us (5%)
  between operations  18.8 us (3%)
    another operation x30, other arithmetic, on_device(): lower = jnp.linalg.cholesky(gram, symmetrize_input=False)  173 us
    all_gather x1, waiting for transfers between devices, on_device(): gram = lax.all_gather(gram_part, 'col', tiled=True)  84.7 us
    another operation x3, other arithmetic, on_device(): factor = jax.scipy.linalg.solve_triangular(lower, rhs, lower=True)  83.5 us
    all_gather x1, waiting for transfers between devices, on_device(): panels = lax.all_gather(mine, 'col')  78.4 us
    all_to_all x1, blocking collectives, on_device(): lax.all_to_all(pieces, 'col', split_axis=0, concat_axis=0, tiled=True)  52.7 us
    psum x1, waiting for transfers between devices, on_device(): rhs = lax.psum(inner_dot(panels, stacked), 'row')  46.4 us
    dot_general x2, matrix products, inner_dot(): return lax.dot_general(left, right, (((0,), (0,)), ((), ())), precision=HI)  23.8 us
    another operation x14, matrix products, on_device(): lower = jnp.linalg.cholesky(gram, symmetrize_input=False)  23.3 us
  transfers between devices with their start and end apart: 3, of which 3 were waited for; matrix products, arithmetic and copies ran while one was open for 0% of the time, Pallas kernels for 0%

commit v1 on v0

--- a/solution.py
+++ b/solution.py
@@ -38,7 +38,9 @@
     share = lead // n_col
     own = lax.dynamic_slice(panels, (0, col_index * share), (height, share))
     gram_part = lax.psum(inner_dot(own, panels), "row")
-    gram = lax.all_gather(gram_part, "col", tiled=True)
+    gram = jnp.concatenate(
+        lax.all_to_all(jnp.stack([gram_part] * lax.axis_size("col")), "col", 0, 0), axis=0
+    )
     rhs = lax.psum(inner_dot(panels, stacked), "row")
     lower = jnp.linalg.cholesky(gram, symmetrize_input=False)
     factor = jax.scipy.linalg.solve_triangular(lower, rhs, lower=True)

time: 647 us -> 675 us (1.043)
  starting transfers between devices: 0.09 us -> 12 us
  waiting for transfers between devices: 210 us -> 221 us
    all_to_all x0 -> x1, waiting for transfers between devices: none -> 95.8 us  [on_device(): lax.all_to_all(jnp.stack([gram_part] * lax.axis_size('col')), 'col', 0, 0)]
    all_gather x1 -> x0, waiting for transfers between devices: 84.7 us -> none  [on_device(): gram = lax.all_gather(gram_part, 'col', tiled=True)]
    all_to_all x0 -> x1, starting transfers between devices: none -> 12 us  [on_device(): lax.all_to_all(jnp.stack([gram_part] * lax.axis_size('col')), 'col', 0, 0)]
    another operation x24 -> x25, local copies, waits for them, and re-layouts: 22.8 us -> 26.2 us
where the time goes in v1:
time: 675 us; the launch traced here: 664 us
  other arithmetic  261 us (39%)
  waiting for transfers between devices  221 us (33%)
  matrix products  60 us (9%)
  blocking collectives  52.7 us (8%)
  local copies, waits for them, and re-layouts  38.1 us (6%)
  between operations  19.1 us (3%)
  starting transfers between devices  12 us (2%)
    another operation x30, other arithmetic, on_device(): lower = jnp.linalg.cholesky(gram, symmetrize_input=False)  173 us
    all_to_all x1, waiting for transfers between devices, on_device(): lax.all_to_all(jnp.stack([gram_part] * lax.axis_size('col')), 'col', 0, 0)  95.8 us
    another operation x3, other arithmetic, on_device(): factor = jax.scipy.linalg.solve_triangular(lower, rhs, lower=True)  83.6 us
    all_gather x1, waiting for transfers between devices, on_device(): panels = lax.all_gather(mine, 'col')  78.4 us
    all_to_all x1, blocking collectives, on_device(): lax.all_to_all(pieces, 'col', split_axis=0, concat_axis=0, tiled=True)  52.7 us
    psum x1, waiting for transfers between devices, on_device(): rhs = lax.psum(inner_dot(panels, stacked), 'row')  46.4 us
    dot_general x2, matrix products, inner_dot(): return lax.dot_general(left, right, (((0,), (0,)), ((), ())), precision=HI)  24.6 us
    another operation x14, matrix products, on_device(): lower = jnp.linalg.cholesky(gram, symmetrize_input=False)  23.3 us
  transfers between devices with their start and end apart: 3, of which 3 were waited for; matrix products, arithmetic and copies ran while one was open for 0% of the time, Pallas kernels for 0%

profile of v1, /device:TPU:1, one launch (start us, length us, event | category | flops | bytes accessed | tf_op | source)
XLA Modules:
  0.0 664.0 jit_solution(102291230653934204)
XLA Ops:
  7.3 1.4 broadcast_multiply_fusion
  8.7 2.1 pad_maximum_fusion
  10.8 1.4 reshape.95
  12.2 52.7 %all_to_all.10 = f32[64,20,256]{2,1,0:T(8,128)S(1)} all-to-all(f32[64,20,256]{2,1,0:T(8,128)S(1)} %reshape.95), channel_id=1, replica_groups=mesh['col'=64,'row'=4] {'col'}, dimensions={0} | all-to-all | bytes 2621440 | tf_op jit(solution)/shard_map/all_to_all | solution.py:34
  65.7 78.4 %all-gather.3.cloned.1.call-done = f32[256,20,256]{2,1,0:T(8,128)} async-done(((f32[4,20,256]{2,1,0:T(8,128)}), f32[256,20,256]{2,1,0:T(8,128)}) %all-gather.3.cloned.1.call-update) | async-done | bytes 5242896 | tf_op jit(solution)/shard_map/all_gather | solution.py:36
  144.1 5.2 copy.5
  149.2 1.3 copy.6
  150.5 9.5 %fusion.63 = f32[1024,256]{1,0:T(8,128)} fusion(f32[1280,1024]{1,0:T(8,128)S(1)} %bitcast.109, f32[1024,256]{1,0:T(8,128)S(1)} %broadcast_multiply_fusion, f32[256,256]{1,0:T(8,128)S(1)} %copy-done), kind=kOutput, calls=%fused_computation.162 | convolution fusion | flops 4026859520 | bytes 7602176 | tf_op jit(solution)/shard_map/dot_general | solution.py:13
  160.1 15.1 %fusion.5 = f32[16,1024]{1,0:T(8,128)} fusion(f32[1280,1024]{1,0:T(8,128)S(1)} %bitcast.110, s32[]{:T(128)S(6)} %select_n.14), kind=kOutput, calls=%fused_computation.31 | convolution fusion | flops 251658240 | bytes 5963780 | tf_op jit(solution)/shard_map/dot_general | solution.py:13
  175.2 46.4 %all-reduce.4.cloned.1.call-done = (f32[1024,256]{1,0:T(8,128)}, f32[16,1024]{1,0:T(8,128)}) async-done(((f32[1024,256]{1,0:T(8,128)}, f32[16,1024]{1,0:T(8,128)}), (f32[1024,256]{1,0:T(8,128)}, f32[16,1024]{1,0:T(8,128)})) %all-reduce.4.cloned.1.call-update) | async-done | bytes 1114128 | tf_op jit(solution)/shard_map/psum | solution.py:44
  221.6 3.3 stack.2
  224.9 12.0 %all-to-all-start.1 = ((f32[64,16,1024]{2,1,0:T(8,128)}), f32[64,16,1024]{2,1,0:T(8,128)}, u32[]{:S(2)}, u32[]{:S(2)}) async-start(f32[64,16,1024]{2,1,0:T(8,128)} %stack.2), calls=%async_computation.1 | async-start | bytes 8388608 | tf_op jit(solution)/shard_map/all_to_all | solution.py:42
  236.9 95.8 %all-to-all-done.1 = f32[64,16,1024]{2,1,0:T(8,128)} async-done(((f32[64,16,1024]{2,1,0:T(8,128)}), f32[64,16,1024]{2,1,0:T(8,128)}, u32[]{:S(2)}, u32[]{:S(2)}) %all-to-all-start.1) | async-done | bytes 4194336 | tf_op jit(solution)/shard_map/all_to_all | solution.py:42
  332.8 0.8 cholesky.580
  333.6 11.7 %cholesky.223 = f32[128,128]{1,0:T(8,128)S(1)} custom-call(f32[128,128]{1,0:T(8,128)S(1)} %cholesky.580), custom_call_target="Cholesky" | custom-call | tf_op jit(solution)/shard_map/jit(cholesky)/cholesky | solution.py:45
  345.4 9.8 %custom-call.63 = f32[1,128,128]{1,2,0:T(8,128)S(1)} custom-call(f32[1,128,128]{2,1,0:T(8,128)S(1)} %get-tuple-element.71), custom_call_target="InvertDiagBlocksLowerTriangular" | custom-call | tf_op jit(solution)/shard_map/jit(cholesky)/cholesky | solution.py:45
  355.2 2.5 cholesky.255
  357.7 2.4 constant_dynamic-update-slice_fusion.31
  360.1 1.5 convolution_subtract_fusion
  361.6 11.7 %cholesky.244 = f32[128,128]{1,0:T(8,128)S(1)} custom-call(f32[128,128]{1,0:T(8,128)S(1)} %cholesky.584), custom_call_target="Cholesky" | custom-call | tf_op jit(solution)/shard_map/jit(cholesky)/cholesky | solution.py:45
  374.0 10.2 %custom-call.64 = f32[1,128,128]{1,2,0:T(8,128)S(1)} custom-call(f32[1,128,128]{2,1,0:T(8,128)S(1)} %get-tuple-element.68), custom_call_target="InvertDiagBlocksLowerTriangular" | custom-call | tf_op jit(solution)/shard_map/jit(cholesky)/cholesky | solution.py:45
  384.2 1.2 convolution_dynamic-update-slice_fusion
  385.4 2.1 convolution_subtract_fusion.1
  387.5 11.7 %cholesky.468 = f32[128,128]{1,0:T(8,128)S(1)} custom-call(f32[128,128]{1,0:T(8,128)S(1)} %cholesky.589), custom_call_target="Cholesky" | custom-call | tf_op jit(solution)/shard_map/jit(cholesky)/cholesky | solution.py:45
  400.6 9.8 %custom-call.65 = f32[1,128,128]{1,2,0:T(8,128)S(1)} custom-call(f32[1,128,128]{2,1,0:T(8,128)S(1)} %get-tuple-element.65), custom_call_target="InvertDiagBlocksLowerTriangular" | custom-call | tf_op jit(solution)/shard_map/jit(cholesky)/cholesky | solution.py:45
  410.4 1.2 convolution_dynamic-update-slice_fusion.1
  411.6 2.3 convolution_subtract_fusion.2
  413.9 11.9 %cholesky.487 = f32[128,128]{1,0:T(8,128)S(1)} custom-call(f32[128,128]{1,0:T(8,128)S(1)} %cholesky.594), custom_call_target="Cholesky" | custom-call | tf_op jit(solution)/shard_map/jit(cholesky)/cholesky | solution.py:45
  427.1 9.8 %custom-call.66 = f32[1,128,128]{1,2,0:T(8,128)S(1)} custom-call(f32[1,128,128]{2,1,0:T(8,128)S(1)} %get-tuple-element.62), custom_call_target="InvertDiagBlocksLowerTriangular" | custom-call | tf_op jit(solution)/shard_map/jit(cholesky)/cholesky | solution.py:45
  437.0 1.1 convolution_dynamic-update-slice_fusion.2
  438.1 2.3 convolution_subtract_fusion.3
  440.4 11.7 %cholesky.506 = f32[128,128]{1,0:T(8,128)S(1)} custom-call(f32[128,128]{1,0:T(8,128)S(1)} %cholesky.599), custom_call_target="Cholesky" | custom-call | tf_op jit(solution)/shard_map/jit(cholesky)/cholesky | solution.py:45
  453.5 9.8 %custom-call.67 = f32[1,128,128]{1,2,0:T(8,128)S(1)} custom-call(f32[1,128,128]{2,1,0:T(8,128)S(1)} %get-tuple-element.59), custom_call_target="InvertDiagBlocksLowerTriangular" | custom-call | tf_op jit(solution)/shard_map/jit(cholesky)/cholesky | solution.py:45
  463.3 1.0 convolution_dynamic-update-slice_fusion.3
  464.3 2.5 convolution_subtract_fusion.4
  466.9 11.7 %cholesky.526 = f32[128,128]{1,0:T(8,128)S(1)} custom-call(f32[128,128]{1,0:T(8,128)S(1)} %cholesky.604), custom_call_target="Cholesky" | custom-call | tf_op jit(solution)/shard_map/jit(cholesky)/cholesky | solution.py:45
  479.9 9.8 %custom-call.68 = f32[1,128,128]{1,2,0:T(8,128)S(1)} custom-call(f32[1,128,128]{2,1,0:T(8,128)S(1)} %get-tuple-element.56), custom_call_target="InvertDiagBlocksLowerTriangular" | custom-call | tf_op jit(solution)/shard_map/jit(cholesky)/cholesky | solution.py:45
  489.7 0.9 convolution_dynamic-update-slice_fusion.5
  490.6 2.0 convolution_subtract_fusion.11
  492.7 11.7 %cholesky.546 = f32[128,128]{1,0:T(8,128)S(1)} custom-call(f32[128,128]{1,0:T(8,128)S(1)} %cholesky.609), custom_call_target="Cholesky" | custom-call | tf_op jit(solution)/shard_map/jit(cholesky)/cholesky | solution.py:45
  505.7 10.2 %custom-call.69 = f32[1,128,128]{1,2,0:T(8,128)S(1)} custom-call(f32[1,128,128]{2,1,0:T(8,128)S(1)} %get-tuple-element.53), custom_call_target="InvertDiagBlocksLowerTriangular" | custom-call | tf_op jit(solution)/shard_map/jit(cholesky)/cholesky | solution.py:45
  515.9 0.8 convolution_dynamic-update-slice_fusion.6
  516.7 1.8 convolution_subtract_fusion.13
  518.5 11.7 %cholesky.564 = f32[128,128]{1,0:T(8,128)S(1)} custom-call(f32[128,128]{1,0:T(8,128)S(1)} %convolution_subtract_fusion.13), custom_call_target="Cholesky" | custom-call | tf_op jit(solution)/shard_map/jit(cholesky)/cholesky | solution.py:45
  530.8 0.7 compare_reduce_fusion
  537.3 4.9 select_select_fusion
  542.2 23.0 %while.1 = (s32[]{:T(128)}, f32[1024,1024]{1,0:T(8,128)}, s32[8,2]{0,1:T(2,128)S(1)}, f32[8,128,128]{2,1,0:T(8,128)S(1)}, s32[]{:T(128)}) while((s32[]{:T(128)}, f32[1024,1024]{1,0:T(8,128)}, s32[8,2]{0,1:T(2,128)S(1)}, f32[8,128,128]{2,1,0:T(8,128)S(1)}, s32[]{:T(128)}) %tuple.58), condition=%wide.while_cond, body=%wide.while_body.sunk | while | flops 2 | bytes 131181 | solution.py:46
  542.8 2.3 bitcast_dynamic-update-slice_fusion.2
  545.7 2.3 bitcast_dynamic-update-slice_fusion.2
  548.6 2.3 bitcast_dynamic-update-slice_fusion.2
  551.5 2.3 bitcast_dynamic-update-slice_fusion.2
  554.3 2.3 bitcast_dynamic-update-slice_fusion.2
  557.2 2.3 bitcast_dynamic-update-slice_fusion.2
  560.1 2.3 bitcast_dynamic-update-slice_fusion.2
  563.0 2.2 bitcast_dynamic-update-slice_fusion.2
  565.2 78.8 %custom-call.70 = f32[8,128,128]{1,2,0:T(8,128)S(1)} custom-call(f32[8,128,128]{2,1,0:T(8,128)S(1)} %get-tuple-element.12), custom_call_target="InvertDiagBlocksLowerTriangular" | custom-call | tf_op jit(solution)/shard_map/jit(_solve_triangular)/triangular_solve | solution.py:46
  644.3 1.1 convolution_subtract_fusion.10
  645.7 1.2 convolution_subtract_fusion.8
  647.3 1.3 convolution_subtract_fusion.7
  648.9 1.4 convolution_subtract_fusion.6
  650.6 1.5 convolution_subtract_fusion.5
  652.4 1.5 convolution_subtract_fusion.9
  654.2 1.6 convolution_subtract_fusion.12
  656.2 0.8 dynamic-slice_select_fusion
  (59 shorter events, 17.5 us)
Async XLA Ops:
  6.5 137.5 %all-gather.3.cloned.1.call-start = ((), (), s32[]{:S(2)}) async-start(), calls=%async_computation.2 | async-start | bytes 6389760 | tf_op jit(solution)/shard_map/all_gather | solution.py:36
  65.6 156.0 %all-reduce.4.cloned.1.call-start = ((), (), s32[]{:S(2)}) async-start(), calls=%async_computation.3 | async-start | bytes 2228224 | tf_op jit(solution)/shard_map/psum | solution.py:44
  149.2 1.3 copy-start
  224.9 107.9 %all-to-all-start.1 = ((f32[64,16,1024]{2,1,0:T(8,128)}), f32[64,16,1024]{2,1,0:T(8,128)}, u32[]{:S(2)}, u32[]{:S(2)}) async-start(f32[64,16,1024]{2,1,0:T(8,128)} %stack.2), calls=%async_computation.1 | async-start | bytes 8388608 | tf_op jit(solution)/shard_map/all_to_all | solution.py:42
  537.3 106.7 %copy-start.1 = (f32[1024,256]{1,0:T(8,128)S(1)}, f32[1024,256]{1,0:T(8,128)}, u32[]{:S(2)}) copy-start(f32[1024,256]{1,0:T(8,128)} %get-tuple-element.21) | copy-start | bytes 3145732
Sparse Core Ops, SparseCore 0:
  65.7 78.2 all-gather.2
  175.3 46.2 all-reduce.3
